TPU v7x, 32 devices: a whole 2x2x4 slice. The times are simulated.
32 devices in a mesh: bas: 8 (over y, x, core), aux: 4 (over z).
Axes of the slice: x: 2, y: 2, z: 4, core: 2. Of those that a mesh axis runs over, the one named last changes fastest.
Arguments:
- integrals: bfloat16 [4, 8192, 8192], P('aux', 'bas'), may hold values from -6 to 6
- screen: int32 [4, 64, 64], P('aux', 'bas'), may hold values from 0 to 1, as said below
- coefficients: bfloat16 [8192, 384], P('bas'), may hold values from -0.0625 to 0.0625
- weights: float32 [384], replicated, may hold values from -2 to 2
Outputs:
- exchange: bfloat16 [8192, 8192], P('aux', 'bas')
Inputs may be any that keep to these rules, and one draw needn't show every extreme that they name: `screen`: every block with equal row and column block index is 1; the share of ones differs from row block to row block.
All inputs are finite; a program needn't handle non-finite values.
Results may differ from a plain program's by a relative error of at most 0.018.
Values may be sent and summed in bfloat16 or wider, within the bound.
A program may use at most 128 MiB of HBM per device.

v0:
```python
import math

import jax
import jax.numpy as jnp
from jax import lax
from jax.sharding import PartitionSpec as P

NOCC = 384
BLOCK = 128
AUX_DEV = 1


def spread_2(block, axis, owner):
    block = jnp.where(lax.axis_index(axis) == owner, block, jnp.zeros_like(block))
    return lax.psum(block, axis)


def shards(integrals, screen, coefficients, weights):
    aux_count = integrals.shape[0]
    row_count = integrals.shape[1]
    basis_count = integrals.shape[2]
    occ_count = coefficients.shape[1]
    row_blocks = row_count // BLOCK
    col_blocks = basis_count // BLOCK
    masks = screen.reshape(aux_count, row_blocks, 1, col_blocks, 1).astype(jnp.bfloat16)
    masked = integrals.reshape(aux_count, row_blocks, BLOCK, col_blocks, BLOCK) * masks
    flat = masked.reshape(aux_count * row_count, basis_count)
    summed_half = jnp.dot(
        flat,
        lax.all_gather(coefficients, "bas", axis=0, tiled=True),
        preferred_element_type=jnp.float32,
    )
    half = summed_half.reshape(aux_count, row_count, occ_count).transpose(1, 0, 2)
    half = half.reshape(row_count, aux_count * occ_count).astype(jnp.bfloat16)
    aux_groups = lax.axis_size("aux")
    scale = 1.0 / math.sqrt(AUX_DEV * aux_groups * NOCC)
    every = lax.all_gather(half, "aux", axis=1, tiled=True)
    weighted_all = (every.astype(jnp.float32) * jnp.tile(weights, aux_count * aux_groups)).astype(
        jnp.bfloat16
    )
    spread = lax.axis_size("bas") // aux_groups
    first = lax.axis_index("aux") * spread
    received = [spread_2(every, "bas", first + offset) for offset in range(spread)]
    owned = jnp.concatenate(received, axis=0)
    per_group = aux_count * occ_count
    left = owned.reshape(owned.shape[0], aux_groups, per_group)
    right = weighted_all.reshape(row_count, aux_groups, per_group)
    terms = jnp.einsum("ngk,mgk->gnm", left, right, preferred_element_type=jnp.float32)
    rounded = lax.optimization_barrier(terms.astype(jnp.bfloat16))
    total = jnp.sum(rounded.astype(jnp.float32), axis=0)
    return (total * scale).astype(jnp.bfloat16)


def solution(mesh):
    in_specs = (P("aux", "bas", None), P("aux", "bas", None), P("bas", None), P())
    out_specs = P("aux", "bas")
    return jax.shard_map(shards, mesh=mesh, in_specs=in_specs, out_specs=out_specs, check_vma=False)
```

profile of v0, /device:TPU:3, one launch (start us, length us, event | category | flops | bytes accessed | tf_op | source)
XLA Modules:
  0.0 301.3 jit_solution(3715893133542091083)
XLA Ops:
  6.5 0.0 all-gather.3.cloned.1.call-start
  6.5 0.7 all-gather.3.cloned.1.call-update
  7.3 0.0 all-gather.5.cloned.1.call-start
  7.3 0.7 convert_bitcast_fusion
  8.0 48.3 %all-gather.3.cloned.1.call-done = bf16[8192,384]{1,0:T(8,128)(2,1)} async-done(((bf16[1024,384]{1,0:T(8,128)(2,1)}), bf16[8192,384]{1,0:T(8,128)(2,1)}) %all-gather.3.cloned.1.call-update) | async-done | bytes 6291472 | tf_op jit(solution)/shard_map/all_gather | solution.py:30
  56.3 6.5 %mul.33 = bf16[8,128,64,128]{3,2,1,0:T(8,128)(2,1)} broadcast(bf16[8,64]{1,0:T(8,128)(2,1)S(1)} %convert_bitcast_fusion), dimensions={0,2} | broadcast | bytes 16778240 | tf_op jit(solution)/shard_map/mul | solution.py:26
  62.7 26.9 %fusion.7 = bf16[1024,384]{1,0:T(8,128)(2,1)} fusion(bf16[8192,384]{1,0:T(8,128)(2,1)} %all-gather.3.cloned.1.call-done, bf16[128,8,64,128]{3,2,1,0:T(8,128)(2,1)} %bitcast.25, bf16[1,1024,8192]{2,1,0:T(8,128)(2,1)} %param.4), kind=kOutput, calls=%fused_computation.15 | convolution fusion | flops 6451232768 | bytes 40632320 | tf_op jit(solution)/shard_map/dot_general | solution.py:28
  89.6 0.0 all-gather.5.cloned.1.call-update
  89.6 0.2 all-reduce.3.cloned.1.call-start
  89.9 0.0 copy-start.2
  89.9 62.5 %all-gather.5.cloned.1.call-done = bf16[1024,1536]{1,0:T(8,128)(2,1)} async-done(((bf16[1024,384]{1,0:T(8,128)(2,1)}), bf16[1024,1536]{1,0:T(8,128)(2,1)}) %all-gather.5.cloned.1.call-update) | async-done | bytes 3145744 | tf_op jit(solution)/shard_map/all_gather | solution.py:37
  152.4 0.0 copy-start
  152.4 5.2 %broadcast_select_fusion.1 = (bf16[1024,1536]{1,0:T(8,128)(2,1)}, bf16[1024,1536]{1,0:T(8,128)(2,1)}) fusion(bf16[1024,1536]{1,0:T(8,128)(2,1)} %all-gather.5.cloned.1.call-done, pred[]{:T(512)S(6)} %eq.6, pred[]{:T(512)S(6)} %eq.7), kind=kLoop, calls=%fused_computation.14 | loop fusion | flops 3145728 | bytes 9437186 | tf_op jit(solution)/shard_map/jit(_where)/select_n | solution.py:14
  157.6 0.0 all-reduce.3.cloned.1.call-update
  157.6 0.0 copy-done.2
  157.7 0.0 copy-done
  157.7 2.3 multiply_convert_fusion.1
  159.9 100.3 %all-reduce.3.cloned.1.call-done = (bf16[1024,1536]{1,0:T(8,128)(2,1)}, bf16[1024,1536]{1,0:T(8,128)(2,1)}) async-done(((bf16[1024,1536]{1,0:T(8,128)(2,1)}, bf16[1024,1536]{1,0:T(8,128)(2,1)}), (bf16[1024,1536]{1,0:T(8,128)(2,1)}, bf16[1024,1536]{1,0:T(8,128)(2,1)})) %all-reduce.3.cloned.1.call-update) | async-done | bytes 6291472 | tf_op jit(solution)/shard_map/psum | solution.py:15
  260.2 0.0 copy-start.1
  260.2 6.1 %pad_maximum_fusion = bf16[2048,1536]{1,0:T(8,128)(2,1)} fusion(bf16[1024,1536]{1,0:T(8,128)(2,1)} %get-tuple-element.5, bf16[1024,1536]{1,0:T(8,128)(2,1)} %get-tuple-element.6), kind=kLoop, calls=%fused_computation.9 | loop fusion | flops 12582912 | bytes 12582912 | tf_op jit(solution)/shard_map/concatenate | solution.py:44
  266.3 0.0 copy-done.1
  266.3 15.3 %convolution_convert_fusion = bf16[4,2048,1024]{2,1,0:T(8,128)(2,1)} fusion(bf16[256,4,8,384]{3,2,1,0:T(8,128)(2,1)} %bitcast.26, bf16[128,4,8,384]{3,2,1,0:T(8,128)(2,1)S(1)} %bitcast.27), kind=kOutput, calls=%fused_computation.5 | convolution fusion | flops 6450839552 | bytes 26214400 | tf_op jit(solution)/shard_map/ngk,mgk->gnm/dot_general | solution.py:48
  281.6 9.8 %convert_reduce_fusion = f32[2048,1024]{1,0:T(8,128)S(1)} fusion(bf16[4,2048,1024]{2,1,0:T(8,128)(2,1)} %convolution_convert_fusion), kind=kLoop, calls=%fused_computation | loop fusion | flops 14680064 | bytes 25165824 | tf_op jit(solution)/shard_map/reduce_sum | solution.py:50
  291.4 3.4 %multiply_convert_fusion = bf16[2048,1024]{1,0:T(8,128)(2,1)} fusion(f32[2048,1024]{1,0:T(8,128)S(1)} %convert_reduce_fusion), kind=kLoop, calls=%fused_computation.6 | loop fusion | flops 4194304 | bytes 12582912 | tf_op jit(solution)/shard_map/convert_element_type | solution.py:51
  (2 shorter events, 0.0 us)
Async XLA Ops:
  6.5 49.7 %all-gather.3.cloned.1.call-start = ((), (), s32[]{:S(2)}) async-start(), calls=%async_computation | async-start | bytes 7077888 | tf_op jit(solution)/shard_map/all_gather | solution.py:30
  7.3 145.2 %all-gather.5.cloned.1.call-start = ((), (), s32[]{:S(2)}) async-start(), calls=%async_computation.1 | async-start | bytes 3932160 | tf_op jit(solution)/shard_map/all_gather | solution.py:37
  89.6 170.6 %all-reduce.3.cloned.1.call-start = ((), (), s32[]{:S(2)}) async-start(), calls=%async_computation.2 | async-start | bytes 12582912 | tf_op jit(solution)/shard_map/psum | solution.py:15
  89.9 67.8 %copy-start.2 = (f32[384]{0:T(512)S(1)}, f32[384]{0:T(512)}, u32[]{:S(2)}) copy-start(f32[384]{0:T(512)} %param.7) | copy-start | bytes 4612
  152.4 5.2 %copy-start = (bf16[1024,1536]{1,0:T(8,128)(2,1)S(1)}, bf16[1024,1536]{1,0:T(8,128)(2,1)}, u32[]{:S(2)}) copy-start(bf16[1024,1536]{1,0:T(8,128)(2,1)} %all-gather.5.cloned.1.call-done) | copy-start | bytes 9437188
  260.2 6.1 %copy-start.1 = (bf16[1024,1536]{1,0:T(8,128)(2,1)S(1)}, bf16[1024,1536]{1,0:T(8,128)(2,1)}, u32[]{:S(2)}) copy-start(bf16[1024,1536]{1,0:T(8,128)(2,1)} %multiply_convert_fusion.1) | copy-start | bytes 9437188
Sparse Core Ops, SparseCore 0:
  9.2 47.0 all-gather.2
  89.7 62.6 all-gather.4
  157.7 102.4 all-reduce.2
where the time goes:
time: 303 us; the launch traced here: 301 us
  waiting for transfers between devices  212 us (70%)
  matrix products  42.1 us (14%)
  other arithmetic  27.4 us (9%)
  between operations  13.2 us (4%)
  local copies, waits for them, and re-layouts  6.49 us (2%)
    psum x1, waiting for transfers between devices, spread_2(): return lax.psum(block, axis)  100 us
    all_gather x1, waiting for transfers between devices, shards(): every = lax.all_gather(half, 'aux', axis=1, tiled=True)  62.5 us
    all_gather x1, waiting for transfers between devices, shards(): lax.all_gather(coefficients, 'bas', axis=0, tiled=True)  48.3 us
    dot_general x1, matrix products, shards(): jnp.dot(flat, lax.all_gather(coefficients, 'bas', axis=0, tiled=True), pr...  26.9 us
    dot_general x1, matrix products, shards(): jnp.einsum('ngk,mgk->gnm', left, right, preferred_element_type=jnp.float32)  15.3 us
    reduce_sum x1, other arithmetic, shards(): total = jnp.sum(rounded.astype(jnp.float32), axis=0)  9.83 us
    mul x1, local copies, waits for them, and re-layouts, shards(): integrals.reshape(aux_count, row_blocks, BLOCK, col_blocks, BLOCK) * masks  6.46 us
  transfers between devices with their start and end apart: 3, of which 3 were waited for; matrix products, arithmetic and copies ran while one was open for 1% of the time, Pallas kernels for 0%

commit v1 on v0

v1 whole, which is shorter than its diff:
```python
import functools
import math

import jax
import jax.numpy as jnp
from jax import lax
from jax.experimental import pallas as pl
from jax.experimental.pallas import tpu as pltpu
from jax.sharding import PartitionSpec as P

BLOCK = 128
LANES = 128


def kernel(groups, aux, scale, integrals, screen, coefs, weights, out,
           ints, fac, acc, right, left, wt, total, result,
           load_sem, ring_send, ring_recv, pair_send, pair_recv,
           line_recv, up_send, down_send,
           lring_send, lring_recv, lpair_send, lpair_recv, lown_sem, out_sem):
    rows, basis = ints.shape
    chunks = fac.shape[0]
    half_rows = rows // 2
    spread = left.shape[1]
    sets = spread // 2
    row_blocks = rows // BLOCK
    col_blocks = basis // BLOCK
    bas_me = lax.axis_index("bas")
    z = lax.axis_index("aux")
    core = bas_me % 2
    half_ring = groups // 2

    def swap(index):
        upper = index // half_ring
        return index + upper * (3 * half_ring - 1 - 2 * index)

    pos = swap(bas_me // 2)

    def device_at(position, which):
        return 2 * swap(position % groups) + which

    partner = bas_me - core + (1 - core)

    def ring_to(half):
        return device_at(pos + groups + 1 - 2 * half, core)

    def remote(src, dst, send, recv, bas=None, aux_to=None):
        return pltpu.make_async_remote_copy(
            src_ref=src, dst_ref=dst, send_sem=send, recv_sem=recv,
            device_id={"bas": bas_me if bas is None else bas, "aux": z if aux_to is None else aux_to},
            device_id_type=pl.DeviceIdType.MESH)

    finish = []

    load_groups = 8
    load_cols = basis // load_groups

    def int_load(i):
        cols = pl.ds(i * load_cols, load_cols)
        return pltpu.make_async_copy(integrals.at[0, :, cols], ints.at[:, cols], load_sem.at[chunks + i])

    def fac_load(j):
        return pltpu.make_async_copy(coefs.at[:, pl.ds(j * LANES, LANES)], fac.at[j, bas_me], load_sem.at[j])

    for j in range(chunks):
        fac_load(j).start()
    for i in range(load_groups):
        int_load(i).start()

    barrier = pltpu.get_barrier_semaphore()
    for other in (ring_to(0), ring_to(1), partner):
        pl.semaphore_signal(barrier, inc=1, device_id={"bas": other, "aux": z}, device_id_type=pl.DeviceIdType.MESH)

    @pl.when(z > 0)
    def _():
        pl.semaphore_signal(barrier, inc=1, device_id={"bas": bas_me, "aux": z - 1}, device_id_type=pl.DeviceIdType.MESH)

    @pl.when(z < aux - 1)
    def _():
        pl.semaphore_signal(barrier, inc=1, device_id={"bas": bas_me, "aux": z + 1}, device_id_type=pl.DeviceIdType.MESH)

    peers = 3 + (z + aux - 1) // aux + (2 * aux - 2 - z) // aux
    pl.semaphore_wait(barrier, peers)

    def origin(h, half, which):
        return device_at(pos + groups - h + 2 * h * half, which)

    def fac_piece(j, h, half, which):
        return fac.at[j, origin(h, half, which), pl.ds(half * half_rows, half_rows)]

    def ring_copy(j, h, half):
        piece = fac_piece(j, h, half, core)
        return remote(piece, piece, ring_send.at[j, h, half], ring_recv.at[j, h, half], bas=ring_to(half))

    def pair_copy(j, h, half):
        piece = fac_piece(j, h, half, core)
        return remote(piece, piece, pair_send.at[j, h, half], pair_recv.at[j, h, half], bas=partner)

    def pass_on(j, h, half):
        if h < groups - 1:
            ring_copy(j, h, half).start()
            finish.append(ring_copy(j, h, half).wait_send)
        pair_copy(j, h, half).start()
        finish.append(pair_copy(j, h, half).wait_send)

    def ring_own(j):
        fac_load(j).wait()
        for half in (0, 1):
            pass_on(j, 0, half)

    def ring_step(j, h):
        for half in (0, 1):
            piece = fac_piece(j, h, half, core)
            remote(piece, piece, ring_send.at[j, h - 1, half], ring_recv.at[j, h - 1, half], bas=ring_to(half)).wait_recv()
            pass_on(j, h, half)

    def pair_wait(j, h):
        for half in (0, 1):
            piece = fac_piece(j, h, half, 1 - core)
            remote(piece, piece, pair_send.at[j, h, half], pair_recv.at[j, h, half], bas=partner).wait_recv()

    def mask_group(i):
        int_load(i).wait()
        per = col_blocks // load_groups

        def body(q, carry):
            column = i * per + q
            cols = pl.ds(pl.multiple_of(column * BLOCK, BLOCK), BLOCK)
            for r in range(row_blocks):
                keep = screen[0, r, column].astype(jnp.float32)
                keep = jnp.full((BLOCK, BLOCK), keep, jnp.float32).astype(jnp.bfloat16)
                ints[pl.ds(r * BLOCK, BLOCK), cols] = ints[pl.ds(r * BLOCK, BLOCK), cols] * keep
            return carry

        lax.fori_loop(0, per, body, 0)

    tile_m = min(256, rows)
    fine = half_rows % LANES == 0

    def piece_dot(j, block, start, length, first):
        def body(m, carry):
            at = pl.ds(pl.multiple_of(m * tile_m, tile_m), tile_m)
            cols = pl.ds(pl.multiple_of(block * rows + start, LANES), length)
            part = jnp.dot(ints[at, cols], fac[j, block, pl.ds(start, length), :],
                           preferred_element_type=jnp.float32)
            acc[at, :] = part if first else acc[at, :] + part
            return carry

        lax.fori_loop(0, rows // tile_m, body, 0)

    def half_dots(j, h):
        pair_wait(j, h)
        if fine:
            if h == 0:
                piece_dot(j, bas_me, 0, rows, True)
                piece_dot(j, partner, 0, rows, False)
            else:
                for half in (0, 1):
                    for which in (core, 1 - core):
                        piece_dot(j, origin(h, half, which), half * half_rows, half_rows, False)
        elif h == groups - 1:
            acc[...] = jnp.zeros_like(acc)

            def body(block, carry):
                piece_dot(j, block, 0, rows, False)
                return carry

            lax.fori_loop(0, 2 * groups, body, 0)

    def weigh(j, p):
        values = right[j, p].astype(jnp.float32) * weights[:, pl.ds(j * LANES, LANES)]
        wt[j, pl.ds(pl.multiple_of(p * LANES, LANES), LANES), :] = values.T.astype(jnp.bfloat16)

    def up_copy(j, p):
        return remote(right.at[j, p], right.at[j, p], up_send.at[j, p], line_recv.at[j, p], aux_to=z + 1)

    def down_copy(j, p):
        return remote(right.at[j, p], right.at[j, p], down_send.at[j, p], line_recv.at[j, p], aux_to=z - 1)

    def guard(condition, action):
        pl.when(condition)(lambda: action())

    def send_up(j, p, condition):
        condition = condition & (z < aux - 1)
        guard(condition, lambda: up_copy(j, p).start())
        finish.append(lambda: guard(condition, lambda: up_copy(j, p).wait_send()))

    def send_down(j, p, condition):
        condition = condition & (z > 0)
        guard(condition, lambda: down_copy(j, p).start())
        finish.append(lambda: guard(condition, lambda: down_copy(j, p).wait_send()))

    def left_piece(ref_index, half):
        j, s, p = ref_index
        return left.at[j, s, p, pl.ds(half * half_rows, half_rows)]

    def lring_copy(src, j, t, p, half):
        return remote(src, left_piece((j, 2 * t + core, p), half),
                      lring_send.at[j, t, p, half], lring_recv.at[j, t, p, half], bas=ring_to(half))

    def lpair_copy(src, j, t, p, half):
        return remote(src, left_piece((j, 2 * t + core, p), half),
                      lpair_send.at[j, t, p, half], lpair_recv.at[j, t, p, half], bas=partner)

    def lown_copy(j, t, p):
        return pltpu.make_async_copy(right.at[j, p], left.at[j, 2 * t + core, p], lown_sem.at[j, t, p])

    def away(t):
        return (pos - swap(z * sets + t) + groups) % groups

    def left_start(j, p, condition):
        for t in range(sets):
            mine = condition & (away(t) == 0)

            def go(t=t):
                for half in (0, 1):
                    src = right.at[j, p, pl.ds(half * half_rows, half_rows)]
                    lring_copy(src, j, t, p, half).start()
                    lpair_copy(src, j, t, p, half).start()
                lown_copy(j, t, p).start()

            def end(t=t):
                for half in (0, 1):
                    src = right.at[j, p, pl.ds(half * half_rows, half_rows)]
                    lring_copy(src, j, t, p, half).wait_send()
                    lpair_copy(src, j, t, p, half).wait_send()

            guard(mine, go)
            finish.append(lambda mine=mine, end=end: guard(mine, end))

    def left_step(j, p, condition):
        for t in range(sets):
            distance = away(t)
            near = (2 * distance) // (groups + 1)
            other = condition & (distance != 0)
            mine = condition & (distance == 0)
            for half in (near, 1 - near):
                hops = distance + half * (groups - 2 * distance)
                src = left_piece((j, 2 * t + core, p), half)

                def go(t=t, half=half, src=src):
                    lring_copy(src, j, t, p, half).wait_recv()
                    lpair_copy(src, j, t, p, half).start()

                def onward(t=t, half=half, src=src):
                    lring_copy(src, j, t, p, half).start()

                def end(t=t, half=half, src=src):
                    lpair_copy(src, j, t, p, half).wait_send()

                def end_onward(t=t, half=half, src=src):
                    lring_copy(src, j, t, p, half).wait_send()

                further = other & (hops < groups - 1)
                guard(other, go)
                guard(further, onward)
                finish.append(lambda other=other, end=end: guard(other, end))
                finish.append(lambda further=further, end=end_onward: guard(further, end))

            def own(t=t):
                lown_copy(j, t, p).wait()

            guard(mine, own)

            def from_partner(t=t):
                for half in (0, 1):
                    dst = left_piece((j, 2 * t + 1 - core, p), half)
                    remote(dst, dst, lpair_send.at[j, t, p, half], lpair_recv.at[j, t, p, half], bas=partner).wait_recv()

            guard(condition, from_partner)

    always = z >= 0

    def members(d):
        if d == 0:
            return [(z, always)]
        return [(z - d, z - d >= 0), (z + d, z + d < aux)]

    def line_event(j, d):
        for p, there in members(d):
            if d == 0:
                send_up(j, p, there)
                send_down(j, p, there)
            elif p is not None:
                guard(there, lambda p=p: up_copy(j, p).wait_recv())
        if d > 0:
            below, above = members(d)
            send_up(j, below[0], below[1])
            send_down(j, above[0], above[1])
        for p, there in members(d):
            left_start(j, p, there)
        if d > 0:
            for p, there in members(d):
                guard(there, lambda p=p: weigh(j, p))

    def left_event(j, d):
        for p, there in members(d):
            left_step(j, p, there)

    def close_half(j):
        right[j, z] = acc[...].astype(jnp.bfloat16)
        weigh(j, z)
        line_event(j, 0)

    tile_n = min(256, rows)
    tiles_in = rows // tile_n
    tiles = spread * tiles_in

    def out_copy(i):
        at = pl.ds(i * tile_n, tile_n)
        return pltpu.make_async_copy(result.at[at], out.at[at], out_sem.at[i])

    def exchange(j, low, high):
        def body(i, carry):
            s, r = i // tiles_in, i % tiles_in
            at = pl.ds(pl.multiple_of(r * tile_n, tile_n), tile_n)
            lhs = jnp.concatenate([left[j, s, p, at, :] for p in range(aux)], axis=1)
            part = jnp.dot(lhs, wt[j], preferred_element_type=jnp.float32)
            to = pl.ds(pl.multiple_of(i * tile_n, tile_n), tile_n)
            if j > 0:
                part = total[to, :] + part
            if j == chunks - 1:
                result[to, :] = (part * scale).astype(jnp.bfloat16)
            else:
                total[to, :] = part
            return carry

        lax.fori_loop(low, high, body, 0)

    ring_own(0)
    if chunks > 1:
        ring_own(1)
    for i in range(load_groups // 2):
        mask_group(i)
    ring_step(0, 1)
    for i in range(load_groups // 2, load_groups):
        mask_group(i)
    for h in range(1, groups):
        if h > 1:
            ring_step(0, h)
        if h == groups - 1 and chunks > 2:
            ring_own(2)
        if chunks > 1:
            ring_step(1, h)
        half_dots(0, h - 1)
    half_dots(0, groups - 1)
    close_half(0)
    events = []
    for j in range(chunks):
        for d in range(1, aux):
            events.append((j, d))
    for j in range(1, chunks):
        for h in range(groups):
            half_dots(j, h)
            if j + 1 < chunks and h + 1 < groups:
                ring_step(j + 1, h + 1)
        close_half(j)
        if j + 2 < chunks:
            ring_own(j + 2)
    behind = [(j, d) for j in range(chunks) for d in range(aux)]
    work = []
    for n, (j, d) in enumerate(events):
        line_event(j, d)
        while behind and behind[0] < (j, d):
            entry = behind.pop(0)
            left_event(*entry)
            if entry[1] == aux - 1:
                step = -(-tiles // max(1, aux - 1))
                work += [(entry[0], low, min(tiles, low + step)) for low in range(0, tiles, step)]
        if work:
            exchange(*work.pop(0))
    while behind:
        left_event(*behind.pop(0))
    for item in work:
        exchange(*item)
    parts = 4 if tiles % 4 == 0 else 1
    for i in range(parts):
        low, high = i * tiles // parts, (i + 1) * tiles // parts
        exchange(chunks - 1, low, high)
        if i > 0:
            for n in range((i - 1) * tiles // parts, low):
                out_copy(n).start()
    for n in range((parts - 1) * tiles // parts, tiles):
        out_copy(n).start()
    for action in finish:
        action()
    for n in range(tiles):
        out_copy(n).wait()


def shards(integrals, screen, coefficients, weights):
    _, rows, basis = integrals.shape
    occ = coefficients.shape[1]
    bas, aux = lax.axis_size("bas"), lax.axis_size("aux")
    groups, spread, chunks = bas // 2, bas // aux, occ // LANES
    sets = spread // 2
    tiles = spread * rows // min(256, rows)
    scale = 1.0 / math.sqrt(integrals.shape[0] * aux * occ)
    dma = pltpu.SemaphoreType.DMA
    bf16, f32 = jnp.bfloat16, jnp.float32
    return pl.pallas_call(
        functools.partial(kernel, groups, aux, scale),
        out_shape=jax.ShapeDtypeStruct((spread * rows, rows), bf16),
        in_specs=[
            pl.BlockSpec(memory_space=pl.ANY),
            pl.BlockSpec(memory_space=pltpu.SMEM),
            pl.BlockSpec(memory_space=pl.ANY),
            pl.BlockSpec(memory_space=pltpu.VMEM),
        ],
        out_specs=pl.BlockSpec(memory_space=pl.ANY),
        scratch_shapes=[
            pltpu.VMEM((rows, basis), bf16),
            pltpu.VMEM((chunks, bas, rows, LANES), bf16),
            pltpu.VMEM((rows, LANES), f32),
            pltpu.VMEM((chunks, aux, rows, LANES), bf16),
            pltpu.VMEM((chunks, spread, aux, rows, LANES), bf16),
            pltpu.VMEM((chunks, aux * LANES, rows), bf16),
            pltpu.VMEM((spread * rows, rows), f32),
            pltpu.VMEM((spread * rows, rows), bf16),
            dma((chunks + 8,)),
            dma((chunks, groups, 2)), dma((chunks, groups, 2)),
            dma((chunks, groups, 2)), dma((chunks, groups, 2)),
            dma((chunks, aux)), dma((chunks, aux)), dma((chunks, aux)),
            dma((chunks, sets, aux, 2)), dma((chunks, sets, aux, 2)),
            dma((chunks, sets, aux, 2)), dma((chunks, sets, aux, 2)),
            dma((chunks, sets, aux)),
            dma((tiles,)),
        ],
        compiler_params=pltpu.CompilerParams(
            collective_id=0, has_side_effects=True, vmem_limit_bytes=62 * 1024 * 1024),
    )(integrals, screen, coefficients, weights.reshape(1, occ))


def solution(mesh):
    in_specs = (P("aux", "bas", None), P("aux", "bas", None), P("bas", None), P())
    out_specs = P("aux", "bas")
    return jax.shard_map(shards, mesh=mesh, in_specs=in_specs, out_specs=out_specs, check_vma=False)
```

time: 303 us -> 206 us (0.68)
  waiting for transfers between devices: 212 us -> 0 us
  Pallas kernels: 0 us -> 200 us
  matrix products: 42.1 us -> 0 us
  other arithmetic: 27.4 us -> 0 us
  between operations: 13.2 us -> 0.01 us
    pallas_call x0 -> x1, Pallas kernels: none -> 200 us  [shards(): pl.pallas_call(functools.partial(kernel, groups, aux, scale), out_shape=j...]
    all_gather x2 -> x0, waiting for transfers between devices: 111 us -> none  [the longest x1 62.5 us: shards(): every = lax.all_gather(half, 'aux', axis=1, tiled=True)]
    psum x1 -> x0, waiting for transfers between devices: 100 us -> none  [spread_2(): return lax.psum(block, axis)]
    dot_general x2 -> x0, matrix products: 42.1 us -> none  [the longest x1 26.9 us: shards(): jnp.dot(flat, lax.all_gather(coefficients, 'bas', axis=0, tiled=True), pr...]
    reduce_sum x1 -> x0, other arithmetic: 9.83 us -> none  [shards(): total = jnp.sum(rounded.astype(jnp.float32), axis=0)]
    mul x2 -> x0, local copies, waits for them, and re-layouts: 6.47 us -> none  [the longest x1 6.46 us: shards(): integrals.reshape(aux_count, row_blocks, BLOCK, col_blocks, BLOCK) * masks]
    convert_element_type x3 -> x0, other arithmetic: 6.33 us -> none  [the longest x1 3.36 us: shards(): return (total * scale).astype(jnp.bfloat16)]
    concatenate x1 -> x0, other arithmetic: 6.06 us -> none  [shards(): owned = jnp.concatenate(received, axis=0)]
  transfers between devices with their start and end apart: 3 -> 0, of which waited for: 3 -> 0; matrix products, arithmetic and copies ran while one was open for 1% -> 0% of each run, Pallas kernels for 0% -> 0%
where the time goes in v1:
time: 206 us; the launch traced here: 205 us
  Pallas kernels  200 us (97%)
  local copies, waits for them, and re-layouts  5.89 us (3%)
    pallas_call x1, Pallas kernels, shards(): pl.pallas_call(functools.partial(kernel, groups, aux, scale), out_shape=j...  200 us
    unnamed x1, local copies, waits for them, and re-layouts  4.64 us

profile of v1, /device:TPU:3, one launch (start us, length us, event | category | flops | bytes accessed | tf_op | source)
XLA Modules:
  0.0 205.4 jit_solution(1917054946948978068)
XLA Ops:
  0.0 1.2 reshape.3.weights
  1.2 199.5 %shard_map.46 = bf16[2048,1024]{1,0:T(8,128)(2,1)} custom-call(bf16[1,1024,8192]{2,1,0:T(8,128)(2,1)} %integrals.1, s32[1,8,64]{2,1,0:T(8,128)} %screen.1, bf16[1024,384]{1,0:T(8,128)(2,1)} %coefs.1, f32[1,384]{1,0:T(1,128)} %reshape.3.weights), custom_call_target="tpu_custom_call" | custom-call | tf_op jit(solution)/shard_map/pallas_call | solution.py:400
  200.8 4.6 %copy.6 = bf16[2048,1024]{1,0:T(8,128)(2,1)} copy(bf16[2048,1024]{1,0:T(8,128)(2,1)} %shard_map.46) | data formatting | bytes 8388608

commit v2 on v1

--- a/solution.py
+++ b/solution.py
@@ -142,7 +142,7 @@
             cols = pl.ds(pl.multiple_of(block * rows + start, LANES), length)
             part = jnp.dot(ints[at, cols], fac[j, block, pl.ds(start, length), :],
                            preferred_element_type=jnp.float32)
-            acc[at, :] = part if first else acc[at, :] + part
+            acc[j, at, :] = part if first else acc[j, at, :] + part
             return carry
 
         lax.fori_loop(0, rows // tile_m, body, 0)
@@ -158,7 +158,7 @@
                     for which in (core, 1 - core):
                         piece_dot(j, origin(h, half, which), half * half_rows, half_rows, False)
         elif h == groups - 1:
-            acc[...] = jnp.zeros_like(acc)
+            acc[j] = jnp.zeros(acc.shape[1:], acc.dtype)
 
             def body(block, carry):
                 piece_dot(j, block, 0, rows, False)
@@ -227,13 +227,15 @@
             guard(mine, go)
             finish.append(lambda mine=mine, end=end: guard(mine, end))
 
-    def left_step(j, p, condition):
+    def left_stage(j, p, condition, stage):
         for t in range(sets):
             distance = away(t)
-            near = (2 * distance) // (groups + 1)
+            side = (2 * distance) // (groups + 1)
+            middle = distance == half_ring
             other = condition & (distance != 0)
-            mine = condition & (distance == 0)
-            for half in (near, 1 - near):
+            takes = other & (middle if stage == 1 else distance != half_ring)
+            halves = (0, 1) if stage == 1 else (side if stage == 0 else 1 - side,)
+            for half in halves:
                 hops = distance + half * (groups - 2 * distance)
                 src = left_piece((j, 2 * t + core, p), half)
 
@@ -250,11 +252,15 @@
                 def end_onward(t=t, half=half, src=src):
                     lring_copy(src, j, t, p, half).wait_send()
 
-                further = other & (hops < groups - 1)
-                guard(other, go)
+                further = takes & (hops < groups - 1)
+                guard(takes, go)
                 guard(further, onward)
-                finish.append(lambda other=other, end=end: guard(other, end))
+                finish.append(lambda takes=takes, end=end: guard(takes, end))
                 finish.append(lambda further=further, end=end_onward: guard(further, end))
+
+    def left_close(j, p, condition):
+        for t in range(sets):
+            mine = condition & (away(t) == 0)
 
             def own(t=t):
                 lown_copy(j, t, p).wait()
@@ -292,14 +298,10 @@
             for p, there in members(d):
                 guard(there, lambda p=p: weigh(j, p))
 
-    def left_event(j, d):
-        for p, there in members(d):
-            left_step(j, p, there)
-
     def close_half(j):
-        right[j, z] = acc[...].astype(jnp.bfloat16)
+        right[j, z] = acc[j].astype(jnp.bfloat16)
         weigh(j, z)
-        line_event(j, 0)
+        slot((j, 0))
 
     tile_n = min(256, rows)
     tiles_in = rows // tile_n
@@ -326,6 +328,30 @@
 
         lax.fori_loop(low, high, body, 0)
 
+    ran = []
+    closed = [0] * chunks
+    work = []
+
+    def slot(event):
+        if event is not None:
+            line_event(*event)
+        ran.append(event)
+        n = len(ran) - 1
+        for stage in range(3):
+            if 0 <= n - 1 - stage and ran[n - 1 - stage] is not None:
+                j, d = ran[n - 1 - stage]
+                for p, there in members(d):
+                    left_stage(j, p, there, stage)
+        if n >= 4 and ran[n - 4] is not None:
+            j, d = ran[n - 4]
+            for p, there in members(d):
+                left_close(j, p, there)
+            closed[j] += 1
+            if closed[j] == aux and j < chunks - 1:
+                step = -(-tiles // max(1, aux - 1))
+                work.extend((j, low, min(tiles, low + step)) for low in range(0, tiles, step))
+
+    events = [(j, d) for j in range(chunks) for d in range(1, aux)]
     ring_own(0)
     if chunks > 1:
         ring_own(1)
@@ -334,42 +360,43 @@
     ring_step(0, 1)
     for i in range(load_groups // 2, load_groups):
         mask_group(i)
-    for h in range(1, groups):
+    for h in range(1, groups - 1):
         if h > 1:
             ring_step(0, h)
-        if h == groups - 1 and chunks > 2:
-            ring_own(2)
+        half_dots(0, h - 1)
         if chunks > 1:
             ring_step(1, h)
-        half_dots(0, h - 1)
+            half_dots(1, h - 1)
+    if groups > 2:
+        ring_step(0, groups - 1)
+    if chunks > 2:
+        ring_own(2)
+    half_dots(0, groups - 2)
     half_dots(0, groups - 1)
     close_half(0)
-    events = []
-    for j in range(chunks):
-        for d in range(1, aux):
-            events.append((j, d))
-    for j in range(1, chunks):
-        for h in range(groups):
-            half_dots(j, h)
-            if j + 1 < chunks and h + 1 < groups:
-                ring_step(j + 1, h + 1)
+    if chunks > 1:
+        ring_step(1, groups - 1)
+        half_dots(1, groups - 2)
+        half_dots(1, groups - 1)
+        close_half(1)
+    for j in range(2, chunks):
+        for h in range(1, groups):
+            ring_step(j, h)
+            half_dots(j, h - 1)
+            if h in (half_ring, groups - 1) and events and events[0][0] < j - 1:
+                slot(events.pop(0))
+        if j + 1 < chunks:
+            ring_own(j + 1)
+        half_dots(j, groups - 1)
         close_half(j)
-        if j + 2 < chunks:
-            ring_own(j + 2)
-    behind = [(j, d) for j in range(chunks) for d in range(aux)]
-    work = []
-    for n, (j, d) in enumerate(events):
-        line_event(j, d)
-        while behind and behind[0] < (j, d):
-            entry = behind.pop(0)
-            left_event(*entry)
-            if entry[1] == aux - 1:
-                step = -(-tiles // max(1, aux - 1))
-                work += [(entry[0], low, min(tiles, low + step)) for low in range(0, tiles, step)]
+    for event in events:
+        slot(event)
         if work:
             exchange(*work.pop(0))
-    while behind:
-        left_event(*behind.pop(0))
+    for _ in range(4):
+        if work:
+            exchange(*work.pop(0))
+        slot(None)
     for item in work:
         exchange(*item)
     parts = 4 if tiles % 4 == 0 else 1
@@ -410,7 +437,7 @@
         scratch_shapes=[
             pltpu.VMEM((rows, basis), bf16),
             pltpu.VMEM((chunks, bas, rows, LANES), bf16),
-            pltpu.VMEM((rows, LANES), f32),
+            pltpu.VMEM((chunks, rows, LANES), f32),
             pltpu.VMEM((chunks, aux, rows, LANES), bf16),
             pltpu.VMEM((chunks, spread, aux, rows, LANES), bf16),
             pltpu.VMEM((chunks, aux * LANES, rows), bf16),

time: 206 us -> 116 us (0.56)
  Pallas kernels: 200 us -> 109 us
    pallas_call x1, Pallas kernels: 200 us -> 109 us  [shards(): pl.pallas_call(functools.partial(kernel, groups, aux, scale), out_shape=j...]
where the time goes in v2:
time: 116 us; the launch traced here: 115 us
  Pallas kernels  109 us (94%)
  local copies, waits for them, and re-layouts  5.89 us (5%)
    pallas_call x1, Pallas kernels, shards(): pl.pallas_call(functools.partial(kernel, groups, aux, scale), out_shape=j...  109 us
    unnamed x1, local copies, waits for them, and re-layouts  4.64 us

profile of v2, /device:TPU:3, one launch (start us, length us, event | category | flops | bytes accessed | tf_op | source)
XLA Modules:
  0.0 115.4 jit_solution(17354251755322563039)
XLA Ops:
  0.0 1.2 %reshape.3.weights = f32[1,384]{1,0:T(1,128)} reshape(f32[384]{0:T(512)} %param.7) | data formatting | bytes 3072 | tf_op jit(solution)/shard_map/reshape | solution.py:457
  1.2 109.5 %shard_map.46 = bf16[2048,1024]{1,0:T(8,128)(2,1)} custom-call(bf16[1,1024,8192]{2,1,0:T(8,128)(2,1)} %integrals.1, s32[1,8,64]{2,1,0:T(8,128)} %screen.1, bf16[1024,384]{1,0:T(8,128)(2,1)} %coefs.1, f32[1,384]{1,0:T(1,128)} %reshape.3.weights), custom_call_target="tpu_custom_call" | custom-call | tf_op jit(solution)/shard_map/pallas_call | solution.py:427
  110.7 4.6 %copy.6 = bf16[2048,1024]{1,0:T(8,128)(2,1)} copy(bf16[2048,1024]{1,0:T(8,128)(2,1)} %shard_map.46) | data formatting | bytes 8388608

commit v3 on v2

--- a/solution.py
+++ b/solution.py
@@ -282,17 +282,13 @@
         return [(z - d, z - d >= 0), (z + d, z + d < aux)]
 
     def line_event(j, d):
-        for p, there in members(d):
-            if d == 0:
+        for n, (p, there) in enumerate(members(d)):
+            if d > 0:
+                guard(there, lambda p=p: up_copy(j, p).wait_recv())
+            if d == 0 or n == 0:
                 send_up(j, p, there)
+            if d == 0 or n == 1:
                 send_down(j, p, there)
-            elif p is not None:
-                guard(there, lambda p=p: up_copy(j, p).wait_recv())
-        if d > 0:
-            below, above = members(d)
-            send_up(j, below[0], below[1])
-            send_down(j, above[0], above[1])
-        for p, there in members(d):
             left_start(j, p, there)
         if d > 0:
             for p, there in members(d):

time: 116 us -> 116 us (level)
  no operation moved by 1% of the time
where the time goes in v3:
time: 116 us; the launch traced here: 115 us
  Pallas kernels  109 us (94%)
  local copies, waits for them, and re-layouts  5.89 us (5%)
    pallas_call x1, Pallas kernels, shards(): pl.pallas_call(functools.partial(kernel, groups, aux, scale), out_shape=j...  109 us
    unnamed x1, local copies, waits for them, and re-layouts  4.64 us

profile of v3, /device:TPU:3, one launch (start us, length us, event | category | flops | bytes accessed | tf_op | source)
XLA Modules:
  0.0 115.4 jit_solution(15217753841631142634)
XLA Ops:
  0.0 1.2 %reshape.3.weights = f32[1,384]{1,0:T(1,128)} reshape(f32[384]{0:T(512)} %param.7) | data formatting | bytes 3072 | tf_op jit(solution)/shard_map/reshape | solution.py:453
  1.2 109.5 %shard_map.46 = bf16[2048,1024]{1,0:T(8,128)(2,1)} custom-call(bf16[1,1024,8192]{2,1,0:T(8,128)(2,1)} %integrals.1, s32[1,8,64]{2,1,0:T(8,128)} %screen.1, bf16[1024,384]{1,0:T(8,128)(2,1)} %coefs.1, f32[1,384]{1,0:T(1,128)} %reshape.3.weights), custom_call_target="tpu_custom_call" | custom-call | tf_op jit(solution)/shard_map/pallas_call | solution.py:423
  110.7 4.6 %copy.6 = bf16[2048,1024]{1,0:T(8,128)(2,1)} copy(bf16[2048,1024]{1,0:T(8,128)(2,1)} %shard_map.46) | data formatting | bytes 8388608
